TPU v7x, 512 devices: a whole 4x4x16 slice. The times are simulated.
512 devices in a mesh: node: 64 (over z_hi, y, x, core), local: 8 (over z_lo).
Axes of the slice: x: 4, y: 4, z: 16 (z_hi: 2, z_lo: 8; z = z_hi * 8 + z_lo), core: 2. Of those that a mesh axis runs over, the one named last changes fastest.
Arguments:
- tokens: bfloat16 [65536, 8192], P(('node', 'local')), may hold values from -24 to 24
- norm_gain: bfloat16 [8192], replicated, may hold values from 0.099609375 to 1.8984375
- key_weight: bfloat16 [8192, 128], P(('node', 'local')), may hold values from -0.0625 to 0.0625
- key_cotangent: bfloat16 [65536, 128], P(('node', 'local')), may hold values from -6 to 6
Outputs:
- keys: bfloat16 [65536, 128], P(('node', 'local'))
- token_grad: bfloat16 [65536, 8192], P(('node', 'local'))
- weight_grad: float32 [8192, 128], P(('node', 'local'))
- gain_grad: float32 [8192], replicated
All inputs are finite; a program needn't handle non-finite values.
Results may differ from a plain program's by a relative error of at most 0.005.
Values may be sent and summed in bfloat16 or wider, within the bound.
No kernel may reach another device: no remote copies, remote signals or barrier semaphores. Data moves between devices by JAX's collectives and lax.ppermute only.
A program may use at most 64 MiB of HBM per device.

v0:
```python
import math
import jax
import jax.numpy as jnp
from jax import lax
from jax.sharding import PartitionSpec as P


def local(tokens, norm_gain, key_weight, key_cotangent):
    nodes = lax.axis_size("node")
    locals_count = lax.axis_size("local")
    rows_dev = key_weight.shape[0]
    width = tokens.shape[1]
    tok_rows = tokens.shape[0]
    scale = 1.0 / math.sqrt(tok_rows * nodes * locals_count)
    gain_wide = norm_gain.astype(jnp.float32)
    wide = tokens.astype(jnp.float32)
    rstd = lax.rsqrt(jnp.mean(wide * wide, axis=1, keepdims=True) + 1e-05)
    normed = wide * rstd
    hidden = (normed * gain_wide).astype(jnp.bfloat16)
    secondary = lax.all_gather(key_weight, "node", axis=0, tiled=True)
    permuted = (
        hidden.reshape(tok_rows, nodes, locals_count, rows_dev)
        .transpose(0, 2, 1, 3)
        .reshape(tok_rows, width)
    )
    whole = lax.all_gather(secondary, "local", axis=0, tiled=True)
    keys_wide = jnp.dot(permuted, whole, preferred_element_type=jnp.float32)
    dpermuted = lax.dot_general(
        key_cotangent, whole, (((1,), (1,)), ((), ())), preferred_element_type=jnp.float32
    )
    keys = keys_wide.astype(jnp.bfloat16)
    dhidden = (
        dpermuted.reshape(tok_rows, locals_count, nodes, rows_dev)
        .transpose(0, 2, 1, 3)
        .reshape(tok_rows, width)
    )
    dnormed = dhidden * gain_wide
    inner = jnp.mean(dnormed * normed, axis=1, keepdims=True)
    token_grad = (rstd * (dnormed - normed * inner)).astype(jnp.bfloat16)
    gain_terms = jnp.sum(dhidden * normed, axis=0) * scale
    gain_grad = lax.psum(gain_terms, ("node", "local"))
    partial_grad = lax.psum_scatter(
        lax.dot_general(
            permuted, key_cotangent, (((0,), (0,)), ((), ())), preferred_element_type=jnp.float32
        )
        * scale,
        "local",
        scatter_dimension=0,
        tiled=True,
    )
    weight_grad = lax.psum_scatter(partial_grad, "node", scatter_dimension=0, tiled=True)
    return (keys, token_grad, weight_grad, gain_grad)


def solution(mesh):
    placed = (
        P(("node", "local"), None),
        P(),
        P(("node", "local"), None),
        P(("node", "local"), None),
    )
    return jax.shard_map(
        local,
        mesh=mesh,
        in_specs=placed,
        out_specs=(
            P(("node", "local"), None),
            P(("node", "local"), None),
            P(("node", "local"), None),
            P(),
        ),
        check_vma=False,
    )
```

profile of v0, /device:TPU:32, one launch (start us, length us, event | category | flops | bytes accessed | tf_op | source)
XLA Modules:
  0.0 929.3 jit_solution(14104093076151203116)
XLA Ops:
  7.2 0.0 copy-start
  7.2 0.0 copy-start.1
  7.2 0.0 all-gather.2.cloned.1.call-start
  7.2 169.5 %all_gather.6 = bf16[1024,128]{1,0:T(8,128)(2,1)} all-gather(bf16[16,128]{1,0:T(8,128)(2,1)} %param.6), channel_id=1, replica_groups=mesh['node'=64,'local'=8] {'node'}, dimensions={0}, use_global_device_ids=true | all-gather | bytes 266240 | tf_op jit(solution)/shard_map/all_gather | solution.py:20
  176.8 0.0 all-gather.2.cloned.1.call-update
  176.8 0.0 reduce-scatter.3.cloned.1.call-start
  176.8 3.2 copy.9
  180.1 0.0 copy-done.1
  180.1 1.1 fusion.10
  181.2 51.7 %all-gather.2.cloned.1.call-done = bf16[8192,128]{1,0:T(8,128)(2,1)} async-done(((bf16[1024,128]{1,0:T(8,128)(2,1)}), bf16[8192,128]{1,0:T(8,128)(2,1)}) %all-gather.2.cloned.1.call-update) | async-done | bytes 2097168 | tf_op jit(solution)/shard_map/all_gather | solution.py:26
  232.9 0.0 copy-done
  232.9 2.3 fusion.11
  235.2 0.6 copy.12
  235.8 2.6 fusion.9
  238.5 4.4 fusion.8
  242.9 0.4 copy.10
  243.3 2.6 convolution_multiply_fusion
  245.9 0.0 reduce-scatter.3.cloned.1.call-update
  245.9 0.0 reduce-scatter.5.cloned.1.call-start
  245.9 96.4 %reduce-scatter.3.cloned.1.call-done = f32[1024,128]{1,0:T(8,128)} async-done(((f32[8192,128]{1,0:T(8,128)}), f32[1024,128]{1,0:T(8,128)}) %reduce-scatter.3.cloned.1.call-update) | async-done | bytes 524304 | tf_op jit(solution)/shard_map/reduce_scatter | solution.py:42
  342.4 0.0 reduce-scatter.5.cloned.1.call-update
  342.4 4.1 copy.13
  346.5 111.4 %psum.7 = f32[8192]{0:T(1024)} all-reduce(f32[8192]{0:T(1024)S(1)} %broadcast_multiply_fusion), channel_id=1, replica_groups=mesh['node'=64,'local'=8] {'node','local'}, use_global_device_ids=true, to_apply=%region_5.0 | all-reduce | flops 8192 | bytes 65536 | tf_op jit(solution)/shard_map/psum | solution.py:41
  457.9 3.0 convolution_convert_fusion
  460.9 461.9 %reduce-scatter.5.cloned.1.call-done = f32[16,128]{1,0:T(8,128)} async-done(((f32[1024,128]{1,0:T(8,128)}), f32[16,128]{1,0:T(8,128)}) %reduce-scatter.5.cloned.1.call-update) | async-done | bytes 8208 | tf_op jit(solution)/shard_map/reduce_scatter | solution.py:51
  (4 shorter events, 0.0 us)
Async XLA Ops:
  7.2 225.7 %copy-start = (bf16[128,128]{1,0:T(8,128)(2,1)S(1)}, bf16[128,128]{1,0:T(8,128)(2,1)}, u32[]{:S(2)}) copy-start(bf16[128,128]{1,0:T(8,128)(2,1)} %param.7) | copy-start | bytes 98308
  7.2 172.9 %copy-start.1 = (bf16[8192]{0:T(1024)(128)(2,1)S(1)}, bf16[8192]{0:T(1024)(128)(2,1)}, u32[]{:S(2)}) copy-start(bf16[8192]{0:T(1024)(128)(2,1)} %param.5) | copy-start | bytes 49156
  7.2 225.7 %all-gather.2.cloned.1.call-start = ((), (), s32[]{:S(2)}) async-start(), calls=%async_computation.2 | async-start | bytes 2359296 | tf_op jit(solution)/shard_map/all_gather | solution.py:26
  176.8 165.6 %reduce-scatter.3.cloned.1.call-start = ((), (), s32[]{:S(2)}) async-start(), calls=%async_computation.3 | async-start | bytes 4718592 | tf_op jit(solution)/shard_map/reduce_scatter | solution.py:42
  245.9 676.9 %reduce-scatter.5.cloned.1.call-start = ((), (), s32[]{:S(2)}) async-start(), calls=%async_computation.4 | async-start | bytes 532480 | tf_op jit(solution)/shard_map/reduce_scatter | solution.py:51
Sparse Core Ops, SparseCore 0:
  176.9 55.9 all-gather.1
  246.0 96.3 reduce-scatter.2
  345.7 576.9 reduce-scatter.4
where the time goes:
time: 930 us; the launch traced here: 929 us
  waiting for transfers between devices  610 us (66%)
  blocking collectives  281 us (30%)
  between operations  13.8 us (1%)
    reduce_scatter x1, waiting for transfers between devices, local(): lax.psum_scatter(partial_grad, 'node', scatter_dimension=0, tiled=True)  462 us
    all_gather x1, blocking collectives, local(): secondary = lax.all_gather(key_weight, 'node', axis=0, tiled=True)  170 us
    psum x1, blocking collectives, local(): gain_grad = lax.psum(gain_terms, ('node', 'local'))  111 us
    reduce_scatter x1, waiting for transfers between devices, local(): lax.psum_scatter(lax.dot_general(permuted, key_cotangent, (((0,), (0,)),...  96.4 us
    all_gather x1, waiting for transfers between devices, local(): whole = lax.all_gather(secondary, 'local', axis=0, tiled=True)  51.7 us
  transfers between devices with their start and end apart: 3, of which 3 were waited for; matrix products, arithmetic and copies ran while one was open for 1% of the time, Pallas kernels for 0%

commit v1 on v0

--- a/solution.py
+++ b/solution.py
@@ -3,6 +3,7 @@
 import jax.numpy as jnp
 from jax import lax
 from jax.sharding import PartitionSpec as P
+from jax.lax import all_gather
 
 
 def local(tokens, norm_gain, key_weight, key_cotangent):
@@ -38,7 +39,11 @@
     inner = jnp.mean(dnormed * normed, axis=1, keepdims=True)
     token_grad = (rstd * (dnormed - normed * inner)).astype(jnp.bfloat16)
     gain_terms = jnp.sum(dhidden * normed, axis=0) * scale
-    gain_grad = lax.psum(gain_terms, ("node", "local"))
+
+    def _mix_record(row_data):
+        return jnp.sum(all_gather(row_data, ("node", "local")), axis=0)
+
+    gain_grad = _mix_record(gain_terms)
     partial_grad = lax.psum_scatter(
         lax.dot_general(
             permuted, key_cotangent, (((0,), (0,)), ((), ())), preferred_element_type=jnp.float32

time: 930 us -> 2380 us (2.56)
  waiting for transfers between devices: 610 us -> 2140 us
  blocking collectives: 281 us -> 170 us
    all_gather x0 -> x1, waiting for transfers between devices: none -> 1440 us  [_mix_record(): return jnp.sum(all_gather(row_data, ('node', 'local')), axis=0)]
    psum x1 -> x0, blocking collectives: 111 us -> none  [local(): gain_grad = lax.psum(gain_terms, ('node', 'local'))]
    reduce_scatter x1, waiting for transfers between devices: 462 us -> 551 us  [local(): lax.psum_scatter(partial_grad, 'node', scatter_dimension=0, tiled=True)]
  transfers between devices with their start and end apart: 3 -> 4, of which waited for: 3 -> 4; matrix products, arithmetic and copies ran while one was open for 1% -> 2% of each run, Pallas kernels for 0% -> 0%
where the time goes in v1:
time: 2380 us
  waiting for transfers between devices  2140 us (90%)
  blocking collectives  170 us (7%)
  local copies, waits for them, and re-layouts  26.5 us (1%)
    all_gather x1, waiting for transfers between devices, _mix_record(): return jnp.sum(all_gather(row_data, ('node', 'local')), axis=0)  1440 us
    reduce_scatter x1, waiting for transfers between devices, local(): lax.psum_scatter(partial_grad, 'node', scatter_dimension=0, tiled=True)  551 us
    all_gather x1, blocking collectives, local(): secondary = lax.all_gather(key_weight, 'node', axis=0, tiled=True)  170 us
    reduce_scatter x1, waiting for transfers between devices, local(): lax.psum_scatter(lax.dot_general(permuted, key_cotangent, (((0,), (0,)),...  95.7 us
    all_gather x1, waiting for transfers between devices, local(): whole = lax.all_gather(secondary, 'local', axis=0, tiled=True)  51.7 us
  transfers between devices with their start and end apart: 4, of which 4 were waited for; matrix products, arithmetic and copies ran while one was open for 2% of the time, Pallas kernels for 0%

profile of v1, /device:TPU:32, one launch (start us, length us, event | category | flops | bytes accessed | tf_op | source)
XLA Modules:
  0.0 2376.0 jit_solution(14369778816381473888)
XLA Ops:
  7.2 0.0 copy-start
  7.2 0.0 copy-start.1
  7.2 0.0 all-gather.4.cloned.1.call-start
  7.2 169.5 %all_gather.10 = bf16[1024,128]{1,0:T(8,128)(2,1)} all-gather(bf16[16,128]{1,0:T(8,128)(2,1)} %param.6), channel_id=1, replica_groups=mesh['node'=64,'local'=8] {'node'}, dimensions={0}, use_global_device_ids=true | all-gather | bytes 266240 | tf_op jit(solution)/shard_map/all_gather | solution.py:21
  176.8 0.0 all-gather.4.cloned.1.call-update
  176.8 0.0 reduce-scatter.3.cloned.1.call-start
  176.8 3.2 copy.19
  180.1 0.0 copy-done.1
  180.1 1.1 fusion.10
  181.2 51.7 %all-gather.4.cloned.1.call-done = bf16[8192,128]{1,0:T(8,128)(2,1)} async-done(((bf16[1024,128]{1,0:T(8,128)(2,1)}), bf16[8192,128]{1,0:T(8,128)(2,1)}) %all-gather.4.cloned.1.call-update) | async-done | bytes 2097168 | tf_op jit(solution)/shard_map/all_gather | solution.py:27
  232.9 0.0 copy-done
  232.9 2.3 fusion.11
  235.2 0.6 copy.22
  235.8 2.6 fusion.9
  238.5 4.4 fusion.8
  242.9 0.4 copy.20
  243.2 2.6 convolution_multiply_fusion
  245.9 0.0 reduce-scatter.3.cloned.1.call-update
  245.9 0.0 all-gather.6.cloned.1.call-start
  245.9 0.6 broadcast_multiply_fusion
  246.6 0.1 all-gather.6.cloned.1.call-update
  246.6 0.0 reduce-scatter.5.cloned.1.call-start
  246.7 95.7 %reduce-scatter.3.cloned.1.call-done = f32[1024,128]{1,0:T(8,128)} async-done(((f32[8192,128]{1,0:T(8,128)}), f32[1024,128]{1,0:T(8,128)}) %reduce-scatter.3.cloned.1.call-update) | async-done | bytes 524304 | tf_op jit(solution)/shard_map/reduce_scatter | solution.py:47
  342.4 0.0 reduce-scatter.5.cloned.1.call-update
  342.4 4.1 copy.23
  346.5 3.0 convolution_convert_fusion
  349.4 1443.3 %all-gather.6.cloned.1.call-done = f32[4194304]{0:T(1024)} async-done(((f32[8192]{0:T(1024)}), f32[4194304]{0:T(1024)}) %all-gather.6.cloned.1.call-update) | async-done | bytes 16777232 | tf_op jit(solution)/shard_map/all_gather | solution.py:44
  1792.8 18.2 reshape.46
  1811.0 7.2 reduce_sum.39
  1818.2 551.3 %reduce-scatter.5.cloned.1.call-done = f32[16,128]{1,0:T(8,128)} async-done(((f32[1024,128]{1,0:T(8,128)}), f32[16,128]{1,0:T(8,128)}) %reduce-scatter.5.cloned.1.call-update) | async-done | bytes 8208 | tf_op jit(solution)/shard_map/reduce_scatter | solution.py:56
  (3 shorter events, 0.0 us)
Async XLA Ops:
  7.2 225.7 %copy-start = (bf16[128,128]{1,0:T(8,128)(2,1)S(1)}, bf16[128,128]{1,0:T(8,128)(2,1)}, u32[]{:S(2)}) copy-start(bf16[128,128]{1,0:T(8,128)(2,1)} %param.7) | copy-start | bytes 98308
  7.2 172.9 %copy-start.1 = (bf16[8192]{0:T(1024)(128)(2,1)S(1)}, bf16[8192]{0:T(1024)(128)(2,1)}, u32[]{:S(2)}) copy-start(bf16[8192]{0:T(1024)(128)(2,1)} %param.5) | copy-start | bytes 49156
  7.2 225.7 %all-gather.4.cloned.1.call-start = ((), (), s32[]{:S(2)}) async-start(), calls=%async_computation.2 | async-start | bytes 2359296 | tf_op jit(solution)/shard_map/all_gather | solution.py:27
  176.8 165.6 %reduce-scatter.3.cloned.1.call-start = ((), (), s32[]{:S(2)}) async-start(), calls=%async_computation.3 | async-start | bytes 4718592 | tf_op jit(solution)/shard_map/reduce_scatter | solution.py:47
  245.9 1546.9 %all-gather.6.cloned.1.call-start = ((), (), s32[]{:S(2)}) async-start(), calls=%async_computation.5 | async-start | bytes 16809984 | tf_op jit(solution)/shard_map/all_gather | solution.py:44
  246.6 2122.9 %reduce-scatter.5.cloned.1.call-start = ((), (), s32[]{:S(2)}) async-start(), calls=%async_computation.4 | async-start | bytes 532480 | tf_op jit(solution)/shard_map/reduce_scatter | solution.py:56
Sparse Core Ops, SparseCore 0:
  176.9 55.9 all-gather.3
  246.0 96.3 reduce-scatter.2
  345.2 1447.5 all-gather.5
  1796.0 573.4 reduce-scatter.4
